TPU v7x, 32 devices: a whole 2x2x4 slice. The times are simulated.
32 devices in a mesh: groups: 2 (over y), space: 4 (over z), dp: 2 (over x), ysp: 2 (over core).
Axes of the slice: x: 2, y: 2, z: 4, core: 2. Of those that a mesh axis runs over, the one named last changes fastest.
Arguments:
- inputs: bfloat16 [4, 8, 16, 2048], P(('groups', 'dp'), 'space', 'ysp'), parts along dimension 0, may hold values from -6 to 6
- w_first: float32 [864, 64], replicated, may hold values from -0.21875 to 0.21875
- b_first: float32 [64], replicated, may hold values from -2 to 2
- w_second: float32 [1728, 64], replicated, may hold values from -0.15625 to 0.15625
- b_second: float32 [64], replicated, may hold values from -2 to 2
- cotangent: bfloat16 [4, 8, 16, 4096], P(('groups', 'dp'), 'space', 'ysp'), parts along dimension 0, may hold values from -16 to 16
Outputs:
- output: bfloat16 [4, 8, 16, 4096], P(('groups', 'dp'), 'space', 'ysp'), parts along dimension 0
- input_grad: bfloat16 [4, 8, 16, 2048], P(('groups', 'dp'), 'space', 'ysp'), parts along dimension 0
- grad_w_first: float32 [1728, 64], P('groups'), parts along dimension 0
- grad_b_first: float32 [128], P('groups'), parts along dimension 0
- grad_w_second: float32 [3456, 64], P('groups'), parts along dimension 0
- grad_b_second: float32 [128], P('groups'), parts along dimension 0
There are 2 independent parts, one for each index of `groups`. A program takes and returns all parts, laid end to end along the dimension named above; an argument that names none is the same for every part. Nothing has to cross between parts.
All inputs are finite; a program needn't handle non-finite values.
Results may differ from a plain program's by a relative error of at most 0.0075.
Values may be sent and summed in bfloat16 or wider, within the bound.
No kernel may reach another device: no remote copies, remote signals or barrier semaphores. Data moves between devices by JAX's collectives and lax.ppermute only.
A program may use at most 64 MiB of HBM per device.

v0:
```python
import jax
import jax.numpy as jnp
from jax import lax
from jax.sharding import PartitionSpec as P

C_IN = 32
C_MID = 64
DEPTH = 64


def padded_2(cells, sides, width):
    for axis, dim in sides:
        count = lax.axis_size(axis)
        ends = count - 1
        head = lax.slice_in_dim(cells, 0, width, axis=dim)
        tail = lax.slice_in_dim(cells, cells.shape[dim] - width, cells.shape[dim], axis=dim)
        cells = jnp.concatenate(
            [
                lax.ppermute(tail, axis, [(i, (i + 1) % count) for i in range(ends)]),
                cells,
                lax.ppermute(head, axis, [((i + 1) % count, i) for i in range(ends)]),
            ],
            axis=dim,
        )
    return cells


def columns(padded, chans):
    batch = padded.shape[0]
    wide_x = padded.shape[1] - 2
    wide_y = padded.shape[2] - 2
    cells = padded.reshape(batch, wide_x + 2, wide_y + 2, DEPTH, chans)
    cells = jnp.pad(cells, ((0, 0), (0, 0), (0, 0), (1, 1), (0, 0)))
    pieces = []
    for first in range(3):
        for second in range(3):
            for third in range(3):
                pieces.append(
                    cells[
                        :,
                        first : first + wide_x,
                        second : second + wide_y,
                        third : third + DEPTH,
                        :,
                    ]
                )
    return jnp.concatenate(pieces, axis=-1).reshape(-1, 27 * chans)


def flipped(weights, chans_in, chans_out):
    cube = weights.reshape(3, 3, 3, chans_in, chans_out)[::-1, ::-1, ::-1]
    return jnp.transpose(cube, (0, 1, 2, 4, 3)).reshape(27 * chans_out, chans_in)


def silu_grad(value):
    sig = jax.nn.sigmoid(value)
    return sig * (1.0 + value * (1.0 - sig))


def weight_term(patches, grads):
    return lax.dot_general(
        patches, grads, (((0,), (0,)), ((), ())), preferred_element_type=jnp.float32
    )


def on_device(inputs, w_first, b_first, w_second, b_second, cotangent):
    batch, cells_x, cells_y = (inputs.shape[0], inputs.shape[1], inputs.shape[2])
    w1_round = w_first.astype(jnp.bfloat16)
    w2_round = w_second.astype(jnp.bfloat16)
    in_padded = padded_2(inputs, (("space", 1), ("ysp", 2)), 1)
    first_cols = columns(in_padded, C_IN)
    y_first = jnp.dot(first_cols, w1_round, preferred_element_type=jnp.float32) + b_first
    act_first = (
        jax.nn.silu(y_first).astype(jnp.bfloat16).reshape(batch, cells_x, cells_y, DEPTH * C_MID)
    )
    mid_padded = padded_2(act_first, (("space", 1), ("ysp", 2)), 1)
    second_cols = columns(mid_padded, C_MID)
    y_second = jnp.dot(second_cols, w2_round, preferred_element_type=jnp.float32) + b_second
    output = (
        jax.nn.silu(y_second).astype(jnp.bfloat16).reshape(batch, cells_x, cells_y, DEPTH * C_MID)
    )
    g_second = (cotangent.reshape(-1, C_MID).astype(jnp.float32) * silu_grad(y_second)).astype(
        jnp.bfloat16
    )
    grad_w2 = weight_term(second_cols, g_second)
    grad_b2 = jnp.sum(g_second.astype(jnp.float32), axis=0)
    g2_padded = padded_2(
        g_second.reshape(batch, cells_x, cells_y, DEPTH * C_MID), (("space", 1), ("ysp", 2)), 1
    )
    d_first = jnp.dot(
        columns(g2_padded, C_MID),
        flipped(w2_round, C_MID, C_MID),
        preferred_element_type=jnp.float32,
    )
    g_first = (d_first * silu_grad(y_first)).astype(jnp.bfloat16)
    grad_w1 = weight_term(first_cols, g_first)
    grad_b1 = jnp.sum(g_first.astype(jnp.float32), axis=0)
    g1_padded = padded_2(
        g_first.reshape(batch, cells_x, cells_y, DEPTH * C_MID), (("space", 1), ("ysp", 2)), 1
    )
    d_input = jnp.dot(
        columns(g1_padded, C_MID),
        flipped(w1_round, C_IN, C_MID),
        preferred_element_type=jnp.float32,
    )
    input_grad = d_input.astype(jnp.bfloat16).reshape(batch, cells_x, cells_y, DEPTH * C_IN)
    grad_w1, grad_b1, grad_w2, grad_b2 = lax.psum(
        (grad_w1, grad_b1, grad_w2, grad_b2), ("space", "dp", "ysp")
    )
    return (output, input_grad, grad_w1, grad_b1, grad_w2, grad_b2)


def solution(mesh):
    placed = (
        P(("groups", "dp"), "space", "ysp", None),
        P(),
        P(),
        P(),
        P(),
        P(("groups", "dp"), "space", "ysp", None),
    )
    return jax.shard_map(
        on_device,
        mesh=mesh,
        in_specs=placed,
        out_specs=(
            P(("groups", "dp"), "space", "ysp", None),
            P(("groups", "dp"), "space", "ysp", None),
            P("groups", None),
            P("groups"),
            P("groups", None),
            P("groups"),
        ),
        check_vma=False,
    )
```

profile of v0, /device:TPU:0, one launch (start us, length us, event | category | flops | bytes accessed | tf_op | source)
XLA Modules:
  0.0 233.7 jit_solution(10804659027833530314)
XLA Ops:
  8.0 4.9 %collective-permute-start = (bf16[1,1,8,2048]{3,2,1,0:T(8,128)(2,1)S(1)}, bf16[1,1,8,2048]{3,2,1,0:T(8,128)(2,1)S(1)}, u32[]{:S(2)}, u32[]{:S(2)}) collective-permute-start(bf16[1,1,8,2048]{3,2,1,0:T(8,128)(2,1)S(1)} %get-tuple-element.136), channel_id=1, source_target_pairs={{0,4},{4,8},{8,12},{1,5},{5,9},{9,13},{2,6},{6,10},{10,14},{3,7},{... | collective-permute-start | bytes 98312 | tf_op jit(solution)/shard_map/ppermute | solution.py:19
  15.3 3.4 %collective-permute-done.1 = bf16[1,1,8,2048]{3,2,1,0:T(8,128)(2,1)S(1)} collective-permute-done((bf16[1,1,8,2048]{3,2,1,0:T(8,128)(2,1)S(1)}, bf16[1,1,8,2048]{3,2,1,0:T(8,128)(2,1)S(1)}, u32[]{:S(2)}, u32[]{:S(2)}) %collective-permute-start.1) | collective-permute-done | bytes 32800 | tf_op jit(solution)/shard_map/ppermute | solution.py:21
  27.5 8.3 %concatenate.38 = bf16[1,2,8,64,864]{4,3,1,2,0:T(8,128)(2,1)} concatenate(bf16[1,2,8,64,32]{4,3,1,2,0:T(8,128)(2,1)S(1)} %get-tuple-element.119, bf16[1,2,8,64,32]{4,3,1,2,0:T(8,128)(2,1)S(1)} %get-tuple-element.118, bf16[1,2,8,64,32]{4,3,1,2,0:T(8,128)(2,1)S(1)} %get-tuple-element.94, bf16[1,2,8,64,32]{4,3,1,2,0:T(8,128)(2,1)S(1)} %get-tuple-element.95, ...), dimensions={4} | concatenate | bytes 3538944 | tf_op jit(solution)/shard_map/concatenate | solution.py:47
  39.6 3.5 %collective-permute-start.4 = (bf16[1,1,8,4096]{3,2,1,0:T(8,128)(2,1)S(1)}, bf16[1,1,8,4096]{3,2,1,0:T(8,128)(2,1)S(1)}, u32[]{:S(2)}, u32[]{:S(2)}) collective-permute-start(bf16[1,1,8,4096]{3,2,1,0:T(8,128)(2,1)S(1)} %get-tuple-element.132), channel_id=1, source_target_pairs={{0,4},{4,8},{8,12},{1,5},{5,9},{9,13},{2,6},{6,10},{10,14},{3,7},{... | collective-permute-start | bytes 196616 | tf_op jit(solution)/shard_map/ppermute | solution.py:19
  45.4 4.4 %collective-permute-done.5 = bf16[1,1,8,4096]{3,2,1,0:T(8,128)(2,1)S(1)} collective-permute-done((bf16[1,1,8,4096]{3,2,1,0:T(8,128)(2,1)S(1)}, bf16[1,1,8,4096]{3,2,1,0:T(8,128)(2,1)S(1)}, u32[]{:S(2)}, u32[]{:S(2)}) %collective-permute-start.5) | collective-permute-done | bytes 65568 | tf_op jit(solution)/shard_map/ppermute | solution.py:21
  49.9 1.9 collective-permute-start.6
  57.2 1.9 pad_slice_fusion.36
  60.8 8.8 %concatenate.41 = bf16[1,2,8,64,1728]{4,3,1,2,0:T(8,128)(2,1)} concatenate(bf16[1,2,8,64,64]{4,3,1,2,0:T(8,128)(2,1)} %get-tuple-element.92, bf16[1,2,8,64,64]{4,3,1,2,0:T(8,128)(2,1)} %get-tuple-element.91, bf16[1,2,8,64,64]{4,3,1,2,0:T(8,128)(2,1)} %get-tuple-element.67, bf16[1,2,8,64,64]{4,3,1,2,0:T(8,128)(2,1)} %get-tuple-element.68, ...), dimensions={4} | concatenate | bytes 7077888 | tf_op jit(solution)/shard_map/concatenate | solution.py:47
  69.7 2.4 %copy.30 = bf16[1,2,8,64,1728]{4,3,2,1,0:T(8,128)(2,1)S(1)} copy(bf16[1,2,8,64,1728]{4,3,1,2,0:T(8,128)(2,1)} %concatenate.41) | data formatting | bytes 7077888 | tf_op jit(solution)/shard_map/concatenate | solution.py:47
  72.2 2.0 convert_reduce_fusion
  75.4 3.5 %collective-permute-start.8 = (bf16[1,1,8,4096]{3,2,1,0:T(8,128)(2,1)S(1)}, bf16[1,1,8,4096]{3,2,1,0:T(8,128)(2,1)S(1)}, u32[]{:S(2)}, u32[]{:S(2)}) collective-permute-start(bf16[1,1,8,4096]{3,2,1,0:T(8,128)(2,1)S(1)} %get-tuple-element.130), channel_id=1, source_target_pairs={{0,4},{4,8},{8,12},{1,5},{5,9},{9,13},{2,6},{6,10},{10,14},{3,7},{... | collective-permute-start | bytes 196616 | tf_op jit(solution)/shard_map/ppermute | solution.py:19
  81.2 4.4 %collective-permute-done.9 = bf16[1,1,8,4096]{3,2,1,0:T(8,128)(2,1)S(1)} collective-permute-done((bf16[1,1,8,4096]{3,2,1,0:T(8,128)(2,1)S(1)}, bf16[1,1,8,4096]{3,2,1,0:T(8,128)(2,1)S(1)}, u32[]{:S(2)}, u32[]{:S(2)}) %collective-permute-start.9) | collective-permute-done | bytes 65568 | tf_op jit(solution)/shard_map/ppermute | solution.py:21
  86.3 1.9 collective-permute-start.10
  97.2 1.8 pad_slice_fusion.18
  100.8 8.8 %concatenate.44 = bf16[1,2,8,64,1728]{4,3,1,2,0:T(8,128)(2,1)} concatenate(bf16[1,2,8,64,64]{4,3,1,2,0:T(8,128)(2,1)} %get-tuple-element.65, bf16[1,2,8,64,64]{4,3,1,2,0:T(8,128)(2,1)} %get-tuple-element.64, bf16[1,2,8,64,64]{4,3,1,2,0:T(8,128)(2,1)} %get-tuple-element.40, bf16[1,2,8,64,64]{4,3,1,2,0:T(8,128)(2,1)} %get-tuple-element.41, ...), dimensions={4} | concatenate | bytes 7077888 | tf_op jit(solution)/shard_map/concatenate | solution.py:47
  109.7 2.4 %copy.35 = bf16[1,2,8,64,1728]{4,3,2,1,0:T(8,128)(2,1)S(1)} copy(bf16[1,2,8,64,1728]{4,3,1,2,0:T(8,128)(2,1)} %concatenate.44) | data formatting | bytes 7077888 | tf_op jit(solution)/shard_map/concatenate | solution.py:47
  114.0 2.3 collective-permute-start.12
  116.3 3.6 %fusion.14 = f32[1728,64]{0,1:T(8,128)} fusion(bf16[1024,64]{0,1:T(8,128)(2,1)S(1)} %copy-done.5, bf16[1024,1728]{1,0:T(8,128)(2,1)} %bitcast.38), kind=kOutput, calls=%fused_computation.114 | convolution fusion | flops 226492416 | bytes 4112384 | tf_op jit(solution)/shard_map/dot_general | solution.py:61
  122.3 5.4 %collective-permute-done.13 = bf16[1,1,8,4096]{3,2,1,0:T(8,128)(2,1)S(1)} collective-permute-done((bf16[1,1,8,4096]{3,2,1,0:T(8,128)(2,1)S(1)}, bf16[1,1,8,4096]{3,2,1,0:T(8,128)(2,1)S(1)}, u32[]{:S(2)}, u32[]{:S(2)}) %collective-permute-start.13) | collective-permute-done | bytes 65568 | tf_op jit(solution)/shard_map/ppermute | solution.py:21
  127.8 1.9 collective-permute-start.14
  132.1 31.3 %all-reduce.4 = (f32[64]{0:T(128)}, f32[64]{0:T(128)}) all-reduce(f32[64]{0:T(128)S(1)} %get-tuple-element.139, f32[64]{0:T(128)S(1)} %get-tuple-element.10), channel_id=1, replica_groups=mesh['groups'=2,'space'=4,'dp'=2,'ysp'=2] {'space','dp','ysp'}, use_global_device_ids=true, to_apply=%region_2.3 | all-reduce | flops 128 | bytes 1024 | tf_op jit(solution)/shard_map/psum | solution.py:107
  168.3 9.0 %concatenate.47 = bf16[1,2,8,64,1728]{4,3,1,2,0:T(8,128)(2,1)} concatenate(bf16[1,2,8,64,64]{4,3,1,2,0:T(8,128)(2,1)} %get-tuple-element.38, bf16[1,2,8,64,64]{4,3,1,2,0:T(8,128)(2,1)} %get-tuple-element.37, bf16[1,2,8,64,64]{4,3,1,2,0:T(8,128)(2,1)S(1)} %get-tuple-element.13, bf16[1,2,8,64,64]{4,3,1,2,0:T(8,128)(2,1)S(1)} %get-tuple-element.14, ...), dimensions={4} | concatenate | bytes 7077888 | tf_op jit(solution)/shard_map/concatenate | solution.py:47
  177.3 2.4 %copy.39 = bf16[1,2,8,64,1728]{4,3,2,1,0:T(8,128)(2,1)S(1)} copy(bf16[1,2,8,64,1728]{4,3,1,2,0:T(8,128)(2,1)} %concatenate.47) | data formatting | bytes 7077888 | tf_op jit(solution)/shard_map/concatenate | solution.py:47
  181.9 41.4 %all-reduce.8.cloned.1.call-done = (f32[864,64]{0,1:T(8,128)}, f32[1728,64]{0,1:T(8,128)}) async-done(((f32[864,64]{0,1:T(8,128)}, f32[1728,64]{0,1:T(8,128)}), (f32[864,64]{0,1:T(8,128)}, f32[1728,64]{0,1:T(8,128)})) %all-reduce.8.cloned.1.call-update) | async-done | bytes 663568 | tf_op jit(solution)/shard_map/psum | solution.py:107
  (123 shorter events, 57.3 us)
Async XLA Ops:
  7.2 216.2 %all-reduce.8.cloned.1.call-start = ((), (), s32[]{:S(2)}) async-start(), calls=%async_computation | async-start | bytes 1376256 | tf_op jit(solution)/shard_map/psum | solution.py:107
  8.0 6.5 %collective-permute-start = (bf16[1,1,8,2048]{3,2,1,0:T(8,128)(2,1)S(1)}, bf16[1,1,8,2048]{3,2,1,0:T(8,128)(2,1)S(1)}, u32[]{:S(2)}, u32[]{:S(2)}) collective-permute-start(bf16[1,1,8,2048]{3,2,1,0:T(8,128)(2,1)S(1)} %get-tuple-element.136), channel_id=1, source_target_pairs={{0,4},{4,8},{8,12},{1,5},{5,9},{9,13},{2,6},{6,10},{10,14},{3,7},{... | collective-permute-start | bytes 98312 | tf_op jit(solution)/shard_map/ppermute | solution.py:19
  12.9 5.8 %collective-permute-start.1 = (bf16[1,1,8,2048]{3,2,1,0:T(8,128)(2,1)S(1)}, bf16[1,1,8,2048]{3,2,1,0:T(8,128)(2,1)S(1)}, u32[]{:S(2)}, u32[]{:S(2)}) collective-permute-start(bf16[1,1,8,2048]{3,2,1,0:T(8,128)(2,1)S(1)} %get-tuple-element.135), channel_id=1, source_target_pairs={{4,0},{8,4},{12,8},{5,1},{9,5},{13,9},{6,2},{10,6},{14,10},{7,3},{... | collective-permute-start | bytes 98312 | tf_op jit(solution)/shard_map/ppermute | solution.py:21
  18.8 4.4 %collective-permute-start.2 = (bf16[1,4,1,2048]{3,2,1,0:T(2,128)(2,1)S(1)}, bf16[1,4,1,2048]{3,2,1,0:T(2,128)(2,1)S(1)}, u32[]{:S(2)}, u32[]{:S(2)}) collective-permute-start(bf16[1,4,1,2048]{3,2,1,0:T(2,128)(2,1)S(1)} %get-tuple-element.133), channel_id=1, source_target_pairs={{0,1},{2,3},{4,5},{6,7},{8,9},{10,11},{12,13},{14,15},{16,17},{18,... | collective-permute-start | bytes 49160 | tf_op jit(solution)/shard_map/ppermute | solution.py:19
  20.1 3.1 %collective-permute-start.3 = (bf16[1,4,1,2048]{3,2,1,0:T(2,128)(2,1)S(1)}, bf16[1,4,1,2048]{3,2,1,0:T(2,128)(2,1)S(1)}, u32[]{:S(2)}, u32[]{:S(2)}) collective-permute-start(bf16[1,4,1,2048]{3,2,1,0:T(2,128)(2,1)S(1)} %get-tuple-element.134), channel_id=1, source_target_pairs={{1,0},{3,2},{5,4},{7,6},{9,8},{11,10},{13,12},{15,14},{17,16},{19,... | collective-permute-start | bytes 49160 | tf_op jit(solution)/shard_map/ppermute | solution.py:21
  35.9 17.2 %copy-start.6 = (f32[1728,64]{0,1:T(8,128)S(1)}, f32[1728,64]{0,1:T(8,128)}, u32[]{:S(2)}) copy-start(f32[1728,64]{0,1:T(8,128)} %param.9) | copy-start | bytes 1327108
  35.9 17.9 %copy-start.10 = (bf16[1,2,8,4096]{3,2,1,0:T(8,128)(2,1)S(1)}, bf16[1,2,8,4096]{3,2,1,0:T(8,128)(2,1)}, u32[]{:S(2)}) copy-start(bf16[1,2,8,4096]{3,2,1,0:T(8,128)(2,1)} %param.11) | copy-start | bytes 393220
  39.6 5.8 %collective-permute-start.4 = (bf16[1,1,8,4096]{3,2,1,0:T(8,128)(2,1)S(1)}, bf16[1,1,8,4096]{3,2,1,0:T(8,128)(2,1)S(1)}, u32[]{:S(2)}, u32[]{:S(2)}) collective-permute-start(bf16[1,1,8,4096]{3,2,1,0:T(8,128)(2,1)S(1)} %get-tuple-element.132), channel_id=1, source_target_pairs={{0,4},{4,8},{8,12},{1,5},{5,9},{9,13},{2,6},{6,10},{10,14},{3,7},{... | collective-permute-start | bytes 196616 | tf_op jit(solution)/shard_map/ppermute | solution.py:19
  43.1 6.7 %collective-permute-start.5 = (bf16[1,1,8,4096]{3,2,1,0:T(8,128)(2,1)S(1)}, bf16[1,1,8,4096]{3,2,1,0:T(8,128)(2,1)S(1)}, u32[]{:S(2)}, u32[]{:S(2)}) collective-permute-start(bf16[1,1,8,4096]{3,2,1,0:T(8,128)(2,1)S(1)} %get-tuple-element.131), channel_id=1, source_target_pairs={{4,0},{8,4},{12,8},{5,1},{9,5},{13,9},{6,2},{10,6},{14,10},{7,3},{... | collective-permute-start | bytes 196616 | tf_op jit(solution)/shard_map/ppermute | solution.py:21
  49.9 5.0 %collective-permute-start.6 = (bf16[1,4,1,4096]{3,2,1,0:T(2,128)(2,1)S(1)}, bf16[1,4,1,4096]{3,2,1,0:T(2,128)(2,1)S(1)}, u32[]{:S(2)}, u32[]{:S(2)}) collective-permute-start(bf16[1,4,1,4096]{3,2,1,0:T(2,128)(2,1)S(1)} %get-tuple-element.125), channel_id=1, source_target_pairs={{0,1},{2,3},{4,5},{6,7},{8,9},{10,11},{12,13},{14,15},{16,17},{18,... | collective-permute-start | bytes 98312 | tf_op jit(solution)/shard_map/ppermute | solution.py:19
  51.8 3.1 %collective-permute-start.7 = (bf16[1,4,1,4096]{3,2,1,0:T(2,128)(2,1)S(1)}, bf16[1,4,1,4096]{3,2,1,0:T(2,128)(2,1)S(1)}, u32[]{:S(2)}, u32[]{:S(2)}) collective-permute-start(bf16[1,4,1,4096]{3,2,1,0:T(2,128)(2,1)S(1)} %get-tuple-element.126), channel_id=1, source_target_pairs={{1,0},{3,2},{5,4},{7,6},{9,8},{11,10},{13,12},{15,14},{17,16},{19,... | collective-permute-start | bytes 98312 | tf_op jit(solution)/shard_map/ppermute | solution.py:21
  69.7 2.5 %copy-start.1 = (bf16[1728,64]{0,1:T(8,128)(2,1)S(1)}, bf16[1728,64]{0,1:T(8,128)(2,1)}, u32[]{:S(2)}) copy-start(bf16[1728,64]{0,1:T(8,128)(2,1)} %convert_element_type.41) | copy-start | bytes 663556
  69.7 2.5 %copy-start.8 = (f32[1024,64]{0,1:T(8,128)S(1)}, f32[1024,64]{0,1:T(8,128)}, u32[]{:S(2)}) copy-start(f32[1024,64]{0,1:T(8,128)} %copy.32) | copy-start | bytes 786436
  72.2 17.5 %copy-start.3 = (bf16[864,64]{1,0:T(8,128)(2,1)S(1)}, bf16[864,64]{1,0:T(8,128)(2,1)}, u32[]{:S(2)}) copy-start(bf16[864,64]{1,0:T(8,128)(2,1)} %copy.27) | copy-start | bytes 331780
  75.4 5.8 %collective-permute-start.8 = (bf16[1,1,8,4096]{3,2,1,0:T(8,128)(2,1)S(1)}, bf16[1,1,8,4096]{3,2,1,0:T(8,128)(2,1)S(1)}, u32[]{:S(2)}, u32[]{:S(2)}) collective-permute-start(bf16[1,1,8,4096]{3,2,1,0:T(8,128)(2,1)S(1)} %get-tuple-element.130), channel_id=1, source_target_pairs={{0,4},{4,8},{8,12},{1,5},{5,9},{9,13},{2,6},{6,10},{10,14},{3,7},{... | collective-permute-start | bytes 196616 | tf_op jit(solution)/shard_map/ppermute | solution.py:19
  78.8 6.7 %collective-permute-start.9 = (bf16[1,1,8,4096]{3,2,1,0:T(8,128)(2,1)S(1)}, bf16[1,1,8,4096]{3,2,1,0:T(8,128)(2,1)S(1)}, u32[]{:S(2)}, u32[]{:S(2)}) collective-permute-start(bf16[1,1,8,4096]{3,2,1,0:T(8,128)(2,1)S(1)} %get-tuple-element.129), channel_id=1, source_target_pairs={{4,0},{8,4},{12,8},{5,1},{9,5},{13,9},{6,2},{10,6},{14,10},{7,3},{... | collective-permute-start | bytes 196616 | tf_op jit(solution)/shard_map/ppermute | solution.py:21
  86.3 8.7 %collective-permute-start.10 = (bf16[1,4,1,4096]{3,2,1,0:T(2,128)(2,1)}, bf16[1,4,1,4096]{3,2,1,0:T(2,128)(2,1)S(1)}, u32[]{:S(2)}, u32[]{:S(2)}) collective-permute-start(bf16[1,4,1,4096]{3,2,1,0:T(2,128)(2,1)} %get-tuple-element.122), channel_id=1, source_target_pairs={{0,1},{2,3},{4,5},{6,7},{8,9},{10,11},{12,13},{14,15},{16,17},{18,... | collective-permute-start | bytes 98312 | tf_op jit(solution)/shard_map/ppermute | solution.py:19
  88.2 6.8 %collective-permute-start.11 = (bf16[1,4,1,4096]{3,2,1,0:T(2,128)(2,1)S(1)}, bf16[1,4,1,4096]{3,2,1,0:T(2,128)(2,1)S(1)}, u32[]{:S(2)}, u32[]{:S(2)}) collective-permute-start(bf16[1,4,1,4096]{3,2,1,0:T(2,128)(2,1)S(1)} %get-tuple-element.123), channel_id=1, source_target_pairs={{1,0},{3,2},{5,4},{7,6},{9,8},{11,10},{13,12},{15,14},{17,16},{19,... | collective-permute-start | bytes 98312 | tf_op jit(solution)/shard_map/ppermute | solution.py:21
  112.1 4.2 %copy-start.5 = (bf16[1024,64]{0,1:T(8,128)(2,1)S(1)}, bf16[1024,64]{0,1:T(8,128)(2,1)}, u32[]{:S(2)}) copy-start(bf16[1024,64]{0,1:T(8,128)(2,1)} %copy-done.4) | copy-start | bytes 393220
  113.5 6.4 %copy-start.11 = (bf16[1024,64]{0,1:T(8,128)(2,1)S(1)}, bf16[1024,64]{0,1:T(8,128)(2,1)}, u32[]{:S(2)}) copy-start(bf16[1024,64]{0,1:T(8,128)(2,1)} %get-tuple-element.124) | copy-start | bytes 393220
  114.0 8.3 %collective-permute-start.12 = (bf16[1,1,8,4096]{3,2,1,0:T(8,128)(2,1)S(1)}, bf16[1,1,8,4096]{3,2,1,0:T(8,128)(2,1)S(1)}, u32[]{:S(2)}, u32[]{:S(2)}) collective-permute-start(bf16[1,1,8,4096]{3,2,1,0:T(8,128)(2,1)S(1)} %get-tuple-element.128), channel_id=1, source_target_pairs={{0,4},{4,8},{8,12},{1,5},{5,9},{9,13},{2,6},{6,10},{10,14},{3,7},{... | collective-permute-start | bytes 196616 | tf_op jit(solution)/shard_map/ppermute | solution.py:19
  121.0 6.7 %collective-permute-start.13 = (bf16[1,1,8,4096]{3,2,1,0:T(8,128)(2,1)S(1)}, bf16[1,1,8,4096]{3,2,1,0:T(8,128)(2,1)S(1)}, u32[]{:S(2)}, u32[]{:S(2)}) collective-permute-start(bf16[1,1,8,4096]{3,2,1,0:T(8,128)(2,1)S(1)} %get-tuple-element.127), channel_id=1, source_target_pairs={{4,0},{8,4},{12,8},{5,1},{9,5},{13,9},{6,2},{10,6},{14,10},{7,3},{... | collective-permute-start | bytes 196616 | tf_op jit(solution)/shard_map/ppermute | solution.py:21
  127.8 35.6 %collective-permute-start.14 = (bf16[1,4,1,4096]{3,2,1,0:T(2,128)(2,1)S(1)}, bf16[1,4,1,4096]{3,2,1,0:T(2,128)(2,1)S(1)}, u32[]{:S(2)}, u32[]{:S(2)}) collective-permute-start(bf16[1,4,1,4096]{3,2,1,0:T(2,128)(2,1)S(1)} %get-tuple-element.120), channel_id=1, source_target_pairs={{0,1},{2,3},{4,5},{6,7},{8,9},{10,11},{12,13},{14,15},{16,17},{18,... | collective-permute-start | bytes 98312 | tf_op jit(solution)/shard_map/ppermute | solution.py:19
  129.7 33.7 %collective-permute-start.15 = (bf16[1,4,1,4096]{3,2,1,0:T(2,128)(2,1)S(1)}, bf16[1,4,1,4096]{3,2,1,0:T(2,128)(2,1)S(1)}, u32[]{:S(2)}, u32[]{:S(2)}) collective-permute-start(bf16[1,4,1,4096]{3,2,1,0:T(2,128)(2,1)S(1)} %get-tuple-element.121), channel_id=1, source_target_pairs={{1,0},{3,2},{5,4},{7,6},{9,8},{11,10},{13,12},{15,14},{17,16},{19,... | collective-permute-start | bytes 98312 | tf_op jit(solution)/shard_map/ppermute | solution.py:21
  (8 other events, 16.2 us)
Sparse Core Ops, SparseCore 0:
  132.2 91.0 all-reduce.7
where the time goes:
time: 237 us; the launch traced here: 234 us
  local copies, waits for them, and re-layouts  82.5 us (35%)
  waiting for transfers between devices  61.4 us (26%)
  starting transfers between devices  31.7 us (13%)
  blocking collectives  31.3 us (13%)
  between operations  14.7 us (6%)
  matrix products  10.6 us (4%)
    concatenate x8, local copies, waits for them, and re-layouts, columns(): return jnp.concatenate(pieces, axis=-1).reshape(-1, 27 * chans)  44 us
    psum x1, waiting for transfers between devices, on_device(): lax.psum((grad_w1, grad_b1, grad_w2, grad_b2), ('space', 'dp', 'ysp'))  41.4 us
    psum x1, blocking collectives, on_device(): lax.psum((grad_w1, grad_b1, grad_w2, grad_b2), ('space', 'dp', 'ysp'))  31.3 us
    ppermute x8, starting transfers between devices, padded_2(): lax.ppermute(tail, axis, [(i, (i + 1) % count) for i in range(ends)])  21.1 us
    ppermute x8, waiting for transfers between devices, padded_2(): lax.ppermute(head, axis, [((i + 1) % count, i) for i in range(ends)])  17.6 us
    slice x12, local copies, waits for them, and re-layouts, columns(): cells[:, first:first + wide_x, second:second + wide_y, third:third + DEPT...  17.1 us
    ppermute x8, starting transfers between devices, padded_2(): lax.ppermute(head, axis, [((i + 1) % count, i) for i in range(ends)])  10.5 us
    unnamed x41, local copies, waits for them, and re-layouts  6.87 us
  transfers between devices with their start and end apart: 17, of which 8 were waited for; matrix products, arithmetic and copies ran while one was open for 15% of the time, Pallas kernels for 0%

commit v1 on v0

--- a/solution.py
+++ b/solution.py
@@ -105,7 +105,7 @@
     )
     input_grad = d_input.astype(jnp.bfloat16).reshape(batch, cells_x, cells_y, DEPTH * C_IN)
     grad_w1, grad_b1, grad_w2, grad_b2 = lax.psum(
-        (grad_w1, grad_b1, grad_w2, grad_b2), ("space", "dp", "ysp")
+        lax.psum((grad_w1, grad_b1, grad_w2, grad_b2), ("dp", "ysp")), "space"
     )
     return (output, input_grad, grad_w1, grad_b1, grad_w2, grad_b2)
 

time: 237 us -> 224 us (0.945)
  blocking collectives: 31.3 us -> 17.1 us
    psum x1 -> x2, blocking collectives: 31.3 us -> 17.1 us  [the longest x1 8.86 us: on_device(): lax.psum(lax.psum((grad_w1, grad_b1, grad_w2, grad_b2), ('dp', 'ysp')), '...]
    psum x1 -> x2, waiting for transfers between devices: 41.4 us -> 41.8 us  [the longest x1 27.6 us: on_device(): lax.psum(lax.psum((grad_w1, grad_b1, grad_w2, grad_b2), ('dp', 'ysp')), '...]
  transfers between devices with their start and end apart: 17 -> 18, of which waited for: 8 -> 9; matrix products, arithmetic and copies ran while one was open for 15% -> 16% of each run, Pallas kernels for 0% -> 0%
where the time goes in v1:
time: 224 us; the launch traced here: 220 us
  local copies, waits for them, and re-layouts  82.6 us (37%)
  waiting for transfers between devices  61.7 us (28%)
  starting transfers between devices  31.7 us (14%)
  blocking collectives  17.1 us (8%)
  between operations  14.7 us (7%)
  matrix products  10.6 us (5%)
    concatenate x8, local copies, waits for them, and re-layouts, columns(): return jnp.concatenate(pieces, axis=-1).reshape(-1, 27 * chans)  44.2 us
    psum x1, waiting for transfers between devices, on_device(): lax.psum(lax.psum((grad_w1, grad_b1, grad_w2, grad_b2), ('dp', 'ysp')), '...  27.6 us
    ppermute x8, starting transfers between devices, padded_2(): lax.ppermute(tail, axis, [(i, (i + 1) % count) for i in range(ends)])  21.1 us
    ppermute x8, waiting for transfers between devices, padded_2(): lax.ppermute(head, axis, [((i + 1) % count, i) for i in range(ends)])  17.6 us
    slice x12, local copies, waits for them, and re-layouts, columns(): cells[:, first:first + wide_x, second:second + wide_y, third:third + DEPT...  17 us
    psum x1, waiting for transfers between devices, on_device(): lax.psum((grad_w1, grad_b1, grad_w2, grad_b2), ('dp', 'ysp'))  14.2 us
    ppermute x8, starting transfers between devices, padded_2(): lax.ppermute(head, axis, [((i + 1) % count, i) for i in range(ends)])  10.5 us
    psum x1, blocking collectives, on_device(): lax.psum(lax.psum((grad_w1, grad_b1, grad_w2, grad_b2), ('dp', 'ysp')), '...  8.86 us
  transfers between devices with their start and end apart: 18, of which 9 were waited for; matrix products, arithmetic and copies ran while one was open for 16% of the time, Pallas kernels for 0%

profile of v1, /device:TPU:0, one launch (start us, length us, event | category | flops | bytes accessed | tf_op | source)
XLA Modules:
  0.0 220.0 jit_solution(1219700791891693101)
XLA Ops:
  8.0 4.9 %collective-permute-start = (bf16[1,1,8,2048]{3,2,1,0:T(8,128)(2,1)S(1)}, bf16[1,1,8,2048]{3,2,1,0:T(8,128)(2,1)S(1)}, u32[]{:S(2)}, u32[]{:S(2)}) collective-permute-start(bf16[1,1,8,2048]{3,2,1,0:T(8,128)(2,1)S(1)} %get-tuple-element.140), channel_id=1, source_target_pairs={{0,4},{4,8},{8,12},{1,5},{5,9},{9,13},{2,6},{6,10},{10,14},{3,7},{... | collective-permute-start | bytes 98312 | tf_op jit(solution)/shard_map/ppermute | solution.py:19
  15.3 3.4 %collective-permute-done.1 = bf16[1,1,8,2048]{3,2,1,0:T(8,128)(2,1)S(1)} collective-permute-done((bf16[1,1,8,2048]{3,2,1,0:T(8,128)(2,1)S(1)}, bf16[1,1,8,2048]{3,2,1,0:T(8,128)(2,1)S(1)}, u32[]{:S(2)}, u32[]{:S(2)}) %collective-permute-start.1) | collective-permute-done | bytes 32800 | tf_op jit(solution)/shard_map/ppermute | solution.py:21
  27.5 8.3 %concatenate.38 = bf16[1,2,8,64,864]{4,3,1,2,0:T(8,128)(2,1)} concatenate(bf16[1,2,8,64,32]{4,3,1,2,0:T(8,128)(2,1)S(1)} %get-tuple-element.123, bf16[1,2,8,64,32]{4,3,1,2,0:T(8,128)(2,1)S(1)} %get-tuple-element.122, bf16[1,2,8,64,32]{4,3,1,2,0:T(8,128)(2,1)S(1)} %get-tuple-element.98, bf16[1,2,8,64,32]{4,3,1,2,0:T(8,128)(2,1)S(1)} %get-tuple-element.99, ...), dimensions={4} | concatenate | bytes 3538944 | tf_op jit(solution)/shard_map/concatenate | solution.py:47
  39.6 3.5 %collective-permute-start.4 = (bf16[1,1,8,4096]{3,2,1,0:T(8,128)(2,1)S(1)}, bf16[1,1,8,4096]{3,2,1,0:T(8,128)(2,1)S(1)}, u32[]{:S(2)}, u32[]{:S(2)}) collective-permute-start(bf16[1,1,8,4096]{3,2,1,0:T(8,128)(2,1)S(1)} %get-tuple-element.136), channel_id=1, source_target_pairs={{0,4},{4,8},{8,12},{1,5},{5,9},{9,13},{2,6},{6,10},{10,14},{3,7},{... | collective-permute-start | bytes 196616 | tf_op jit(solution)/shard_map/ppermute | solution.py:19
  45.4 4.4 %collective-permute-done.5 = bf16[1,1,8,4096]{3,2,1,0:T(8,128)(2,1)S(1)} collective-permute-done((bf16[1,1,8,4096]{3,2,1,0:T(8,128)(2,1)S(1)}, bf16[1,1,8,4096]{3,2,1,0:T(8,128)(2,1)S(1)}, u32[]{:S(2)}, u32[]{:S(2)}) %collective-permute-start.5) | collective-permute-done | bytes 65568 | tf_op jit(solution)/shard_map/ppermute | solution.py:21
  49.9 1.9 collective-permute-start.6
  60.8 8.8 %concatenate.41 = bf16[1,2,8,64,1728]{4,3,1,2,0:T(8,128)(2,1)} concatenate(bf16[1,2,8,64,64]{4,3,1,2,0:T(8,128)(2,1)} %get-tuple-element.96, bf16[1,2,8,64,64]{4,3,1,2,0:T(8,128)(2,1)} %get-tuple-element.95, bf16[1,2,8,64,64]{4,3,1,2,0:T(8,128)(2,1)} %get-tuple-element.71, bf16[1,2,8,64,64]{4,3,1,2,0:T(8,128)(2,1)} %get-tuple-element.72, ...), dimensions={4} | concatenate | bytes 7077888 | tf_op jit(solution)/shard_map/concatenate | solution.py:47
  69.7 2.4 %copy.30 = bf16[1,2,8,64,1728]{4,3,2,1,0:T(8,128)(2,1)S(1)} copy(bf16[1,2,8,64,1728]{4,3,1,2,0:T(8,128)(2,1)} %concatenate.41) | data formatting | bytes 7077888 | tf_op jit(solution)/shard_map/concatenate | solution.py:47
  72.2 2.0 convert_reduce_fusion
  75.4 3.5 %collective-permute-start.8 = (bf16[1,1,8,4096]{3,2,1,0:T(8,128)(2,1)S(1)}, bf16[1,1,8,4096]{3,2,1,0:T(8,128)(2,1)S(1)}, u32[]{:S(2)}, u32[]{:S(2)}) collective-permute-start(bf16[1,1,8,4096]{3,2,1,0:T(8,128)(2,1)S(1)} %get-tuple-element.134), channel_id=1, source_target_pairs={{0,4},{4,8},{8,12},{1,5},{5,9},{9,13},{2,6},{6,10},{10,14},{3,7},{... | collective-permute-start | bytes 196616 | tf_op jit(solution)/shard_map/ppermute | solution.py:19
  81.2 4.4 %collective-permute-done.9 = bf16[1,1,8,4096]{3,2,1,0:T(8,128)(2,1)S(1)} collective-permute-done((bf16[1,1,8,4096]{3,2,1,0:T(8,128)(2,1)S(1)}, bf16[1,1,8,4096]{3,2,1,0:T(8,128)(2,1)S(1)}, u32[]{:S(2)}, u32[]{:S(2)}) %collective-permute-start.9) | collective-permute-done | bytes 65568 | tf_op jit(solution)/shard_map/ppermute | solution.py:21
  86.3 1.9 collective-permute-start.10
  100.8 8.8 %concatenate.44 = bf16[1,2,8,64,1728]{4,3,1,2,0:T(8,128)(2,1)} concatenate(bf16[1,2,8,64,64]{4,3,1,2,0:T(8,128)(2,1)} %get-tuple-element.69, bf16[1,2,8,64,64]{4,3,1,2,0:T(8,128)(2,1)} %get-tuple-element.68, bf16[1,2,8,64,64]{4,3,1,2,0:T(8,128)(2,1)} %get-tuple-element.44, bf16[1,2,8,64,64]{4,3,1,2,0:T(8,128)(2,1)} %get-tuple-element.45, ...), dimensions={4} | concatenate | bytes 7077888 | tf_op jit(solution)/shard_map/concatenate | solution.py:47
  109.7 2.4 %copy.35 = bf16[1,2,8,64,1728]{4,3,2,1,0:T(8,128)(2,1)S(1)} copy(bf16[1,2,8,64,1728]{4,3,1,2,0:T(8,128)(2,1)} %concatenate.44) | data formatting | bytes 7077888 | tf_op jit(solution)/shard_map/concatenate | solution.py:47
  114.0 2.3 %collective-permute-start.12 = (bf16[1,1,8,4096]{3,2,1,0:T(8,128)(2,1)S(1)}, bf16[1,1,8,4096]{3,2,1,0:T(8,128)(2,1)S(1)}, u32[]{:S(2)}, u32[]{:S(2)}) collective-permute-start(bf16[1,1,8,4096]{3,2,1,0:T(8,128)(2,1)S(1)} %get-tuple-element.132), channel_id=1, source_target_pairs={{0,4},{4,8},{8,12},{1,5},{5,9},{9,13},{2,6},{6,10},{10,14},{3,7},{... | collective-permute-start | bytes 196616 | tf_op jit(solution)/shard_map/ppermute | solution.py:19
  116.3 3.6 %fusion.14 = f32[1728,64]{0,1:T(8,128)} fusion(bf16[1024,64]{0,1:T(8,128)(2,1)S(1)} %copy-done.5, bf16[1024,1728]{1,0:T(8,128)(2,1)} %bitcast.38), kind=kOutput, calls=%fused_computation.114 | convolution fusion | flops 226492416 | bytes 4112384 | tf_op jit(solution)/shard_map/dot_general | solution.py:61
  122.3 5.4 %collective-permute-done.13 = bf16[1,1,8,4096]{3,2,1,0:T(8,128)(2,1)S(1)} collective-permute-done((bf16[1,1,8,4096]{3,2,1,0:T(8,128)(2,1)S(1)}, bf16[1,1,8,4096]{3,2,1,0:T(8,128)(2,1)S(1)}, u32[]{:S(2)}, u32[]{:S(2)}) %collective-permute-start.13) | collective-permute-done | bytes 65568 | tf_op jit(solution)/shard_map/ppermute | solution.py:21
  127.8 1.9 collective-permute-start.14
  132.2 8.2 %all-reduce.4 = (f32[64]{0:T(128)S(1)}, f32[64]{0:T(128)S(1)}) all-reduce(f32[64]{0:T(128)S(1)} %get-tuple-element.143, f32[64]{0:T(128)S(1)} %get-tuple-element.14), channel_id=1, replica_groups=mesh['groups'=2,'space'=4,'dp'=2,'ysp'=2] {'dp','ysp'}, use_global_device_ids=true, to_apply=%region_3.4 | all-reduce | flops 128 | bytes 1024 | tf_op jit(solution)/shard_map/psum | solution.py:108
  140.4 8.9 %all-reduce.6 = (f32[64]{0:T(128)}, f32[64]{0:T(128)}) all-reduce(f32[64]{0:T(128)S(1)} %get-tuple-element.6, f32[64]{0:T(128)S(1)} %get-tuple-element.7), channel_id=1, replica_groups=mesh['groups'=2,'space'=4,'dp'=2,'ysp'=2] {'space'}, use_global_device_ids=true, to_apply=%region_4.5 | all-reduce | flops 128 | bytes 1024 | tf_op jit(solution)/shard_map/psum | solution.py:107
  151.1 14.2 %all-reduce.11.cloned.1.call-done = (f32[864,64]{0,1:T(8,128)}, f32[1728,64]{0,1:T(8,128)}) async-done(((f32[864,64]{0,1:T(8,128)}, f32[1728,64]{0,1:T(8,128)}), (f32[864,64]{0,1:T(8,128)}, f32[1728,64]{0,1:T(8,128)})) %all-reduce.11.cloned.1.call-update) | async-done | bytes 663568 | tf_op jit(solution)/shard_map/psum | solution.py:108
  168.2 9.2 %concatenate.47 = bf16[1,2,8,64,1728]{4,3,1,2,0:T(8,128)(2,1)} concatenate(bf16[1,2,8,64,64]{4,3,1,2,0:T(8,128)(2,1)} %get-tuple-element.42, bf16[1,2,8,64,64]{4,3,1,2,0:T(8,128)(2,1)} %get-tuple-element.41, bf16[1,2,8,64,64]{4,3,1,2,0:T(8,128)(2,1)S(1)} %get-tuple-element.17, bf16[1,2,8,64,64]{4,3,1,2,0:T(8,128)(2,1)S(1)} %get-tuple-element.18, ...), dimensions={4} | concatenate | bytes 7077888 | tf_op jit(solution)/shard_map/concatenate | solution.py:47
  177.4 2.4 %copy.39 = bf16[1,2,8,64,1728]{4,3,2,1,0:T(8,128)(2,1)S(1)} copy(bf16[1,2,8,64,1728]{4,3,1,2,0:T(8,128)(2,1)} %concatenate.47) | data formatting | bytes 7077888 | tf_op jit(solution)/shard_map/concatenate | solution.py:47
  182.1 27.6 %all-reduce.13.cloned.1.call-done = (f32[864,64]{0,1:T(8,128)}, f32[1728,64]{0,1:T(8,128)}) async-done(((f32[864,64]{0,1:T(8,128)}, f32[1728,64]{0,1:T(8,128)}), (f32[864,64]{0,1:T(8,128)}, f32[1728,64]{0,1:T(8,128)})) %all-reduce.13.cloned.1.call-update) | async-done | bytes 663568 | tf_op jit(solution)/shard_map/psum | solution.py:107
  (127 shorter events, 61.0 us)
Async XLA Ops:
  7.2 158.1 %all-reduce.11.cloned.1.call-start = ((), (), s32[]{:S(2)}) async-start(), calls=%async_computation | async-start | bytes 1376256 | tf_op jit(solution)/shard_map/psum | solution.py:108
  8.0 6.5 %collective-permute-start = (bf16[1,1,8,2048]{3,2,1,0:T(8,128)(2,1)S(1)}, bf16[1,1,8,2048]{3,2,1,0:T(8,128)(2,1)S(1)}, u32[]{:S(2)}, u32[]{:S(2)}) collective-permute-start(bf16[1,1,8,2048]{3,2,1,0:T(8,128)(2,1)S(1)} %get-tuple-element.140), channel_id=1, source_target_pairs={{0,4},{4,8},{8,12},{1,5},{5,9},{9,13},{2,6},{6,10},{10,14},{3,7},{... | collective-permute-start | bytes 98312 | tf_op jit(solution)/shard_map/ppermute | solution.py:19
  12.9 5.8 %collective-permute-start.1 = (bf16[1,1,8,2048]{3,2,1,0:T(8,128)(2,1)S(1)}, bf16[1,1,8,2048]{3,2,1,0:T(8,128)(2,1)S(1)}, u32[]{:S(2)}, u32[]{:S(2)}) collective-permute-start(bf16[1,1,8,2048]{3,2,1,0:T(8,128)(2,1)S(1)} %get-tuple-element.139), channel_id=1, source_target_pairs={{4,0},{8,4},{12,8},{5,1},{9,5},{13,9},{6,2},{10,6},{14,10},{7,3},{... | collective-permute-start | bytes 98312 | tf_op jit(solution)/shard_map/ppermute | solution.py:21
  18.8 4.4 %collective-permute-start.2 = (bf16[1,4,1,2048]{3,2,1,0:T(2,128)(2,1)S(1)}, bf16[1,4,1,2048]{3,2,1,0:T(2,128)(2,1)S(1)}, u32[]{:S(2)}, u32[]{:S(2)}) collective-permute-start(bf16[1,4,1,2048]{3,2,1,0:T(2,128)(2,1)S(1)} %get-tuple-element.137), channel_id=1, source_target_pairs={{0,1},{2,3},{4,5},{6,7},{8,9},{10,11},{12,13},{14,15},{16,17},{18,... | collective-permute-start | bytes 49160 | tf_op jit(solution)/shard_map/ppermute | solution.py:19
  20.1 3.1 %collective-permute-start.3 = (bf16[1,4,1,2048]{3,2,1,0:T(2,128)(2,1)S(1)}, bf16[1,4,1,2048]{3,2,1,0:T(2,128)(2,1)S(1)}, u32[]{:S(2)}, u32[]{:S(2)}) collective-permute-start(bf16[1,4,1,2048]{3,2,1,0:T(2,128)(2,1)S(1)} %get-tuple-element.138), channel_id=1, source_target_pairs={{1,0},{3,2},{5,4},{7,6},{9,8},{11,10},{13,12},{15,14},{17,16},{19,... | collective-permute-start | bytes 49160 | tf_op jit(solution)/shard_map/ppermute | solution.py:21
  35.9 17.2 %copy-start.6 = (f32[1728,64]{0,1:T(8,128)S(1)}, f32[1728,64]{0,1:T(8,128)}, u32[]{:S(2)}) copy-start(f32[1728,64]{0,1:T(8,128)} %param.9) | copy-start | bytes 1327108
  35.9 17.9 %copy-start.10 = (bf16[1,2,8,4096]{3,2,1,0:T(8,128)(2,1)S(1)}, bf16[1,2,8,4096]{3,2,1,0:T(8,128)(2,1)}, u32[]{:S(2)}) copy-start(bf16[1,2,8,4096]{3,2,1,0:T(8,128)(2,1)} %param.11) | copy-start | bytes 393220
  39.6 5.8 %collective-permute-start.4 = (bf16[1,1,8,4096]{3,2,1,0:T(8,128)(2,1)S(1)}, bf16[1,1,8,4096]{3,2,1,0:T(8,128)(2,1)S(1)}, u32[]{:S(2)}, u32[]{:S(2)}) collective-permute-start(bf16[1,1,8,4096]{3,2,1,0:T(8,128)(2,1)S(1)} %get-tuple-element.136), channel_id=1, source_target_pairs={{0,4},{4,8},{8,12},{1,5},{5,9},{9,13},{2,6},{6,10},{10,14},{3,7},{... | collective-permute-start | bytes 196616 | tf_op jit(solution)/shard_map/ppermute | solution.py:19
  43.1 6.7 %collective-permute-start.5 = (bf16[1,1,8,4096]{3,2,1,0:T(8,128)(2,1)S(1)}, bf16[1,1,8,4096]{3,2,1,0:T(8,128)(2,1)S(1)}, u32[]{:S(2)}, u32[]{:S(2)}) collective-permute-start(bf16[1,1,8,4096]{3,2,1,0:T(8,128)(2,1)S(1)} %get-tuple-element.135), channel_id=1, source_target_pairs={{4,0},{8,4},{12,8},{5,1},{9,5},{13,9},{6,2},{10,6},{14,10},{7,3},{... | collective-permute-start | bytes 196616 | tf_op jit(solution)/shard_map/ppermute | solution.py:21
  49.9 5.0 %collective-permute-start.6 = (bf16[1,4,1,4096]{3,2,1,0:T(2,128)(2,1)S(1)}, bf16[1,4,1,4096]{3,2,1,0:T(2,128)(2,1)S(1)}, u32[]{:S(2)}, u32[]{:S(2)}) collective-permute-start(bf16[1,4,1,4096]{3,2,1,0:T(2,128)(2,1)S(1)} %get-tuple-element.129), channel_id=1, source_target_pairs={{0,1},{2,3},{4,5},{6,7},{8,9},{10,11},{12,13},{14,15},{16,17},{18,... | collective-permute-start | bytes 98312 | tf_op jit(solution)/shard_map/ppermute | solution.py:19
  51.8 3.1 %collective-permute-start.7 = (bf16[1,4,1,4096]{3,2,1,0:T(2,128)(2,1)S(1)}, bf16[1,4,1,4096]{3,2,1,0:T(2,128)(2,1)S(1)}, u32[]{:S(2)}, u32[]{:S(2)}) collective-permute-start(bf16[1,4,1,4096]{3,2,1,0:T(2,128)(2,1)S(1)} %get-tuple-element.130), channel_id=1, source_target_pairs={{1,0},{3,2},{5,4},{7,6},{9,8},{11,10},{13,12},{15,14},{17,16},{19,... | collective-permute-start | bytes 98312 | tf_op jit(solution)/shard_map/ppermute | solution.py:21
  69.7 2.5 %copy-start.1 = (bf16[1728,64]{0,1:T(8,128)(2,1)S(1)}, bf16[1728,64]{0,1:T(8,128)(2,1)}, u32[]{:S(2)}) copy-start(bf16[1728,64]{0,1:T(8,128)(2,1)} %convert_element_type.41) | copy-start | bytes 663556
  72.2 17.5 %copy-start.3 = (bf16[864,64]{1,0:T(8,128)(2,1)S(1)}, bf16[864,64]{1,0:T(8,128)(2,1)}, u32[]{:S(2)}) copy-start(bf16[864,64]{1,0:T(8,128)(2,1)} %copy.27) | copy-start | bytes 331780
  75.4 5.8 %collective-permute-start.8 = (bf16[1,1,8,4096]{3,2,1,0:T(8,128)(2,1)S(1)}, bf16[1,1,8,4096]{3,2,1,0:T(8,128)(2,1)S(1)}, u32[]{:S(2)}, u32[]{:S(2)}) collective-permute-start(bf16[1,1,8,4096]{3,2,1,0:T(8,128)(2,1)S(1)} %get-tuple-element.134), channel_id=1, source_target_pairs={{0,4},{4,8},{8,12},{1,5},{5,9},{9,13},{2,6},{6,10},{10,14},{3,7},{... | collective-permute-start | bytes 196616 | tf_op jit(solution)/shard_map/ppermute | solution.py:19
  78.8 6.7 %collective-permute-start.9 = (bf16[1,1,8,4096]{3,2,1,0:T(8,128)(2,1)S(1)}, bf16[1,1,8,4096]{3,2,1,0:T(8,128)(2,1)S(1)}, u32[]{:S(2)}, u32[]{:S(2)}) collective-permute-start(bf16[1,1,8,4096]{3,2,1,0:T(8,128)(2,1)S(1)} %get-tuple-element.133), channel_id=1, source_target_pairs={{4,0},{8,4},{12,8},{5,1},{9,5},{13,9},{6,2},{10,6},{14,10},{7,3},{... | collective-permute-start | bytes 196616 | tf_op jit(solution)/shard_map/ppermute | solution.py:21
  86.3 8.7 %collective-permute-start.10 = (bf16[1,4,1,4096]{3,2,1,0:T(2,128)(2,1)}, bf16[1,4,1,4096]{3,2,1,0:T(2,128)(2,1)S(1)}, u32[]{:S(2)}, u32[]{:S(2)}) collective-permute-start(bf16[1,4,1,4096]{3,2,1,0:T(2,128)(2,1)} %get-tuple-element.126), channel_id=1, source_target_pairs={{0,1},{2,3},{4,5},{6,7},{8,9},{10,11},{12,13},{14,15},{16,17},{18,... | collective-permute-start | bytes 98312 | tf_op jit(solution)/shard_map/ppermute | solution.py:19
  88.2 6.8 %collective-permute-start.11 = (bf16[1,4,1,4096]{3,2,1,0:T(2,128)(2,1)S(1)}, bf16[1,4,1,4096]{3,2,1,0:T(2,128)(2,1)S(1)}, u32[]{:S(2)}, u32[]{:S(2)}) collective-permute-start(bf16[1,4,1,4096]{3,2,1,0:T(2,128)(2,1)S(1)} %get-tuple-element.127), channel_id=1, source_target_pairs={{1,0},{3,2},{5,4},{7,6},{9,8},{11,10},{13,12},{15,14},{17,16},{19,... | collective-permute-start | bytes 98312 | tf_op jit(solution)/shard_map/ppermute | solution.py:21
  112.1 4.2 %copy-start.5 = (bf16[1024,64]{0,1:T(8,128)(2,1)S(1)}, bf16[1024,64]{0,1:T(8,128)(2,1)}, u32[]{:S(2)}) copy-start(bf16[1024,64]{0,1:T(8,128)(2,1)} %copy-done.4) | copy-start | bytes 393220
  113.5 6.4 %copy-start.11 = (bf16[1024,64]{0,1:T(8,128)(2,1)S(1)}, bf16[1024,64]{0,1:T(8,128)(2,1)}, u32[]{:S(2)}) copy-start(bf16[1024,64]{0,1:T(8,128)(2,1)} %get-tuple-element.128) | copy-start | bytes 393220
  114.0 8.3 %collective-permute-start.12 = (bf16[1,1,8,4096]{3,2,1,0:T(8,128)(2,1)S(1)}, bf16[1,1,8,4096]{3,2,1,0:T(8,128)(2,1)S(1)}, u32[]{:S(2)}, u32[]{:S(2)}) collective-permute-start(bf16[1,1,8,4096]{3,2,1,0:T(8,128)(2,1)S(1)} %get-tuple-element.132), channel_id=1, source_target_pairs={{0,4},{4,8},{8,12},{1,5},{5,9},{9,13},{2,6},{6,10},{10,14},{3,7},{... | collective-permute-start | bytes 196616 | tf_op jit(solution)/shard_map/ppermute | solution.py:19
  121.0 6.7 %collective-permute-start.13 = (bf16[1,1,8,4096]{3,2,1,0:T(8,128)(2,1)S(1)}, bf16[1,1,8,4096]{3,2,1,0:T(8,128)(2,1)S(1)}, u32[]{:S(2)}, u32[]{:S(2)}) collective-permute-start(bf16[1,1,8,4096]{3,2,1,0:T(8,128)(2,1)S(1)} %get-tuple-element.131), channel_id=1, source_target_pairs={{4,0},{8,4},{12,8},{5,1},{9,5},{13,9},{6,2},{10,6},{14,10},{7,3},{... | collective-permute-start | bytes 196616 | tf_op jit(solution)/shard_map/ppermute | solution.py:21
  127.8 21.5 %collective-permute-start.14 = (bf16[1,4,1,4096]{3,2,1,0:T(2,128)(2,1)S(1)}, bf16[1,4,1,4096]{3,2,1,0:T(2,128)(2,1)S(1)}, u32[]{:S(2)}, u32[]{:S(2)}) collective-permute-start(bf16[1,4,1,4096]{3,2,1,0:T(2,128)(2,1)S(1)} %get-tuple-element.124), channel_id=1, source_target_pairs={{0,1},{2,3},{4,5},{6,7},{8,9},{10,11},{12,13},{14,15},{16,17},{18,... | collective-permute-start | bytes 98312 | tf_op jit(solution)/shard_map/ppermute | solution.py:19
  129.7 19.6 %collective-permute-start.15 = (bf16[1,4,1,4096]{3,2,1,0:T(2,128)(2,1)S(1)}, bf16[1,4,1,4096]{3,2,1,0:T(2,128)(2,1)S(1)}, u32[]{:S(2)}, u32[]{:S(2)}) collective-permute-start(bf16[1,4,1,4096]{3,2,1,0:T(2,128)(2,1)S(1)} %get-tuple-element.125), channel_id=1, source_target_pairs={{1,0},{3,2},{5,4},{7,6},{9,8},{11,10},{13,12},{15,14},{17,16},{19,... | collective-permute-start | bytes 98312 | tf_op jit(solution)/shard_map/ppermute | solution.py:21
  132.1 77.6 %all-reduce.13.cloned.1.call-start = ((), (), s32[]{:S(2)}) async-start(), calls=%async_computation.1 | async-start | bytes 1376256 | tf_op jit(solution)/shard_map/psum | solution.py:107
  (9 other events, 18.7 us)
Sparse Core Ops, SparseCore 0:
  132.2 32.9 all-reduce.10
  167.8 41.8 all-reduce.12
